TPU v7x, 32 devices: a whole 2x2x4 slice. The times are simulated.
32 devices in a mesh: gx: 4 (over x, core), gy: 4 (over z), gz: 2 (over y).
Axes of the slice: x: 2, y: 2, z: 4, core: 2. Of those that a mesh axis runs over, the one named last changes fastest.
Arguments:
- loads: bfloat16 [4, 4, 2, 2048, 128], P('gx', 'gy', 'gz'), may hold values from -12 to 12, as said below
- start_guess: bfloat16 [4, 4, 2, 2048, 128], P('gx', 'gy', 'gz'), may hold values from -1.1953125 to 1.1953125
- schur_blocks: bfloat16 [4, 4, 2, 2048, 2048], P('gx', 'gy', 'gz'), may hold values from -1 to 5, as said below
- coupling: bfloat16 [4, 4, 2, 6, 128, 128], P('gx', 'gy', 'gz'), may hold values from -0.25 to 0.25
- diag_inverse: bfloat16 [4, 4, 2, 16, 128, 128], P('gx', 'gy', 'gz'), may hold values from -1 to 1, as said below
- lower_blocks: bfloat16 [4, 4, 2, 15, 128, 128], P('gx', 'gy', 'gz'), may hold values from -0.1875 to 0.1875
- upper_blocks: bfloat16 [4, 4, 2, 15, 128, 128], P('gx', 'gy', 'gz'), may hold values from -0.1875 to 0.1875
Outputs:
- solution: float32 [4, 4, 2, 2048, 128], P('gx', 'gy', 'gz')
- residual_ratio: float32 [128], replicated
Inputs may be any that keep to these rules, and one draw needn't show every extreme that they name: Each subdomain's loads are independent entries times a factor of that subdomain. `schur_blocks`: each subdomain's Schur block has a positive diagonal between 2 and 4 and full independent off-diagonal entries. `diag_inverse`: each block has a positive diagonal between 0.25 and 0.5 and full independent off-diagonal entries.
All inputs are finite; a program needn't handle non-finite values.
Results may differ from a plain program's by a relative error of at most 0.0037.
Values may be sent and summed in bfloat16 or wider, within the bound.
A program may use at most 64 MiB of HBM per device.

v0:
```python
import jax
import jax.numpy as jnp
from jax import lax
from jax.sharding import PartitionSpec as P

U = 2048
F = 128
B = 128
R = 128
ITERS = 2
NB = 16


epsilon = 1e-06


def with_halo(cells, sides, width):
    for axis, dim in sides:
        count = lax.axis_size(axis)
        head = lax.slice_in_dim(cells, 0, width, axis=dim)
        tail = lax.slice_in_dim(cells, cells.shape[dim] - width, cells.shape[dim], axis=dim)
        cells = jnp.concatenate(
            [
                lax.ppermute(tail, axis, [(i, (i + 1) % count) for i in range(count)]),
                cells,
                lax.ppermute(head, axis, [((i + 1) % count, i) for i in range(count)]),
            ],
            axis=dim,
        )
    return cells


def neighbour_faces(face_rows):
    along_x = with_halo(face_rows[0:2][None], (("gx", 0),), 1)
    along_y = with_halo(face_rows[2:4][None], (("gy", 0),), 1)
    along_z = with_halo(face_rows[4:6][None], (("gz", 0),), 1)
    return jnp.stack(
        [along_x[0, 1], along_x[2, 0], along_y[0, 1], along_y[2, 0], along_z[0, 1], along_z[2, 0]]
    )


def operate(values, schur_block, couple_block):
    own_part = jnp.dot(schur_block, values, preferred_element_type=jnp.float32)
    face_rows = values[: 6 * F].reshape(6, F, values.shape[1])
    neighbours = neighbour_faces(face_rows)
    coupled = lax.dot_general(
        couple_block, neighbours, (((2,), (1,)), ((0,), (0,))), preferred_element_type=jnp.float32
    )
    return jnp.concatenate(
        [own_part[: 6 * F] + coupled.reshape(6 * F, R), own_part[6 * F :]], axis=0
    )


def precondition(values, diag_blocks, lower_one, upper_one):
    blocks = values.reshape(NB, B, R)

    def forward(previous, inputs):
        block_in, lower_block = inputs
        current = block_in - jnp.dot(
            lower_block, previous.astype(jnp.bfloat16), preferred_element_type=jnp.float32
        )
        return (current, current)

    carried, remaining = lax.scan(forward, blocks[0], (blocks[1:], lower_one))
    forward_sweep = jnp.concatenate([blocks[0][None], remaining], axis=0)
    final_block = jnp.dot(
        diag_blocks[NB - 1],
        forward_sweep[NB - 1].astype(jnp.bfloat16),
        preferred_element_type=jnp.float32,
    )

    def backward(next_block, inputs):
        block_in, diag_block, upper_block = inputs
        inner = block_in - jnp.dot(
            upper_block, next_block.astype(jnp.bfloat16), preferred_element_type=jnp.float32
        )
        current = jnp.dot(
            diag_block, inner.astype(jnp.bfloat16), preferred_element_type=jnp.float32
        )
        return (current, current)

    carried, earlier = lax.scan(
        backward, final_block, (forward_sweep[:-1], diag_blocks[:-1], upper_one), reverse=True
    )
    return jnp.concatenate([earlier, final_block[None]], axis=0).reshape(U, R)


def least_squares(hessenberg, start_norm):
    columns = hessenberg.shape[1]
    unit_vectors = []
    triangle = {}
    for column in range(columns):
        vector = hessenberg[:, column]
        for earlier in range(column):
            weight = jnp.sum(unit_vectors[earlier] * vector, axis=0)
            triangle[earlier, column] = weight
            vector = vector - weight * unit_vectors[earlier]
        length = jnp.sqrt(jnp.sum(vector * vector, axis=0))
        triangle[column, column] = length
        unit_vectors.append(vector / length)
    target = [start_norm * unit_vectors[column][0] for column in range(columns)]
    coeffs = [None] * columns
    for column in range(columns - 1, -1, -1):
        running = target[column]
        for earlier in range(column + 1, columns):
            running = running - triangle[column, earlier] * coeffs[earlier]
        coeffs[column] = running / triangle[column, column]
    coeffs = jnp.stack(coeffs)
    unit_first = jnp.zeros((columns + 1, 1), jnp.float32).at[0].set(1.0)
    misfit = unit_first * start_norm - jnp.sum(hessenberg * coeffs[None], axis=1)
    return (coeffs, jnp.sqrt(jnp.sum(misfit * misfit, axis=0)) / start_norm)


def body(loads, start_guess, schur_blocks, coupling, diag_inverse, lower_blocks, upper_blocks):
    schur_block = schur_blocks[0, 0, 0]
    couple_block = coupling[0, 0, 0]
    diag_blocks = diag_inverse[0, 0, 0]
    lower_one = lower_blocks[0, 0, 0]
    upper_one = upper_blocks[0, 0, 0]
    warm_start = start_guess[0, 0, 0]
    residual = loads[0, 0, 0].astype(jnp.float32) - operate(warm_start, schur_block, couple_block)
    start_norm = jnp.sqrt(
        lax.psum(jnp.sum(residual * residual, axis=0), ("gx", "gy", "gz")) + epsilon
    )
    krylov = [residual / start_norm]
    hessenberg = jnp.zeros((ITERS + 1, ITERS, R), jnp.float32)
    directions = []
    for column in range(ITERS):
        direction = precondition(krylov[column], diag_blocks, lower_one, upper_one)
        directions.append(direction)
        mapped = operate(direction.astype(jnp.bfloat16), schur_block, couple_block)
        stacked = jnp.stack(krylov)
        own_products = jnp.sum(stacked * mapped[None], axis=1)
        projected, squares = lax.psum(
            (own_products, jnp.sum(mapped * mapped, axis=0)), ("gx", "gy", "gz")
        )
        mapped = mapped - jnp.sum(projected[:, None, :] * stacked, axis=0)
        length = jnp.sqrt(squares - jnp.sum(projected * projected, axis=0) + epsilon)
        hessenberg = (
            hessenberg.at[: column + 1, column].set(projected).at[column + 1, column].set(length)
        )
        if column + 1 < ITERS:
            krylov.append(mapped / length)
    coeffs, residual_ratio = least_squares(hessenberg, start_norm)
    solution = warm_start.astype(jnp.float32)
    for column in range(ITERS):
        solution = solution + coeffs[column] * directions[column]
    return (solution[None, None, None], residual_ratio)


def solution(mesh):
    in_specs = (
        P("gx", "gy", "gz", None, None),
        P("gx", "gy", "gz", None, None),
        P("gx", "gy", "gz", None, None),
        P("gx", "gy", "gz", None, None, None),
        P("gx", "gy", "gz", None, None, None),
        P("gx", "gy", "gz", None, None, None),
        P("gx", "gy", "gz", None, None, None),
    )
    out_specs = (P("gx", "gy", "gz", None, None), P())
    return jax.shard_map(body, mesh=mesh, in_specs=in_specs, out_specs=out_specs, check_vma=False)
```

profile of v0, /device:TPU:0, one launch (start us, length us, event | category | flops | bytes accessed | tf_op | source)
XLA Modules:
  0.0 269.4 jit_solution(9059985981006871884)
XLA Ops:
  2.2 2.0 collective-permute-start.1
  4.2 2.3 collective-permute-start.2
  6.5 2.0 collective-permute-start.3
  8.6 1.7 collective-permute-start.4
  10.3 5.8 %fusion.40 = f32[2048,128]{1,0:T(8,128)S(1)} fusion(bf16[1,1,1,2048,2048]{4,3,2,1,0:T(8,128)(2,1)} %param.27, bf16[1,1,1,2048,128]{4,3,2,1,0:T(8,128)(2,1)} %param.26), kind=kOutput, calls=%fused_computation.40 | convolution fusion | flops 1073741824 | bytes 9961472 | tf_op jit(solution)/shard_map/dot_general | solution.py:43
  18.9 3.9 %collective-permute-done.5 = bf16[1,2,128,128]{3,2,1,0:T(8,128)(2,1)S(1)} collective-permute-done((bf16[1,2,128,128]{3,2,1,0:T(8,128)(2,1)S(1)}, bf16[1,2,128,128]{3,2,1,0:T(8,128)(2,1)S(1)}, u32[]{:S(2)}, u32[]{:S(2)}) %collective-permute-start.5) | collective-permute-done | bytes 65568 | tf_op jit(solution)/shard_map/ppermute | solution.py:26
  23.4 37.7 %psum.35 = f32[128]{0:T(128)S(1)} all-reduce(f32[128]{0:T(128)S(1)} %multiply_reduce_fusion.3), channel_id=1, replica_groups=mesh['gx'=4,'gy'=4,'gz'=2] {'gx','gy','gz'}, use_global_device_ids=true, to_apply=%region_1.0 | all-reduce | flops 128 | bytes 1024 | tf_op jit(solution)/shard_map/psum | solution.py:123
  63.4 15.6 %while.61 = (s32[]{:T(128)}, bf16[128,128]{1,0:T(8,128)(2,1)S(1)}, f32[15,128,128]{2,1,0:T(8,128)S(1)}, f32[15,128,128]{2,1,0:T(8,128)}, bf16[15,128,128]{2,1,0:T(8,128)(2,1)}, /*index=5*/s32[]{:T(128)}) while((s32[]{:T(128)}, bf16[128,128]{1,0:T(8,128)(2,1)S(1)}, f32[15,128,128]{2,1,0:T(8,128)S(1)}, f32[15,128,128]{2,1,0:T(8,128)}, ...), condition=%wide.region_3.4_spmd, body=%wide.region_2.3_spmd.sunk | while | flops 4227074 | bytes 296005 | solution.py:64
  81.0 18.0 %while.62 = (s32[]{:T(128)}, bf16[128,128]{1,0:T(8,128)(2,1)S(1)}, f32[15,128,128]{2,1,0:T(8,128)S(1)}, bf16[15,128,128]{2,1,0:T(8,128)(2,1)}, f32[15,128,128]{2...) while((s32[]{:T(128)}, bf16[128,128]{1,0:T(8,128)(2,1)S(1)}, ...), condition=%wide.region_5.6_spmd, body=%wide.region_4.5_spmd.sunk | while | flops 8437763 | bytes 329825 | solution.py:82
  99.1 1.7 collective-permute-start.7
  100.9 2.0 collective-permute-start.8
  102.8 1.9 collective-permute-start.9
  104.7 5.9 %fusion.42 = f32[2048,128]{1,0:T(8,128)S(1)} fusion(bf16[2048,128]{1,0:T(8,128)(2,1)S(1)} %bitcast.335, bf16[1,1,1,2048,2048]{4,3,2,1,0:T(8,128)(2,1)} %param.27), kind=kOutput, calls=%fused_computation.42 | convolution fusion | flops 1073741824 | bytes 9961472 | tf_op jit(solution)/shard_map/dot_general | solution.py:43
  111.8 2.3 collective-permute-start.10
  114.2 2.8 %collective-permute-done.10 = bf16[1,2,128,128]{3,2,1,0:T(8,128)(2,1)S(1)} collective-permute-done((bf16[1,2,128,128]{3,2,1,0:T(8,128)(2,1)S(1)}, bf16[1,2,128,128]{3,2,1,0:T(8,128)(2,1)S(1)}, u32[]{:S(2)}, u32[]{:S(2)}) %collective-permute-start.10) | collective-permute-done | bytes 65568 | tf_op jit(solution)/shard_map/ppermute | solution.py:24
  116.9 1.4 collective-permute-done.11
  119.2 38.1 %all-reduce.2 = (f32[128]{0:T(128)S(1)}, f32[1,128]{1,0:T(1,128)S(1)}) all-reduce(f32[128]{0:T(128)S(1)} %multiply_reduce_fusion.1, f32[1,128]{1,0:T(1,128)S(1)} %bitcast.351), channel_id=1, replica_groups=mesh['gx'=4,'gy'=4,'gz'=2] {'gx','gy','gz'}, use_global_device_ids=true, to_apply=%region_9.10 | all-reduce | flops 256 | bytes 2048 | tf_op jit(solution)/shard_map/psum | solution.py:134
  157.3 1.3 subtract_divide_fusion
  159.7 15.6 %while.63 = (s32[]{:T(128)}, bf16[128,128]{1,0:T(8,128)(2,1)S(1)}, f32[15,128,128]{2,1,0:T(8,128)S(1)}, f32[15,128,128]{2,1,0:T(8,128)}, bf16[15,128,128]{2,1,0:T(8,128)(2,1)}, /*index=5*/s32[]{:T(128)}) while((s32[]{:T(128)}, bf16[128,128]{1,0:T(8,128)(2,1)S(1)}, f32[15,128,128]{2,1,0:T(8,128)S(1)}, f32[15,128,128]{2,1,0:T(8,128)}, ...), condition=%wide.region_11.12_spmd, body=%wide.region_10.11_spmd.sunk | while | flops 4227074 | bytes 296005 | solution.py:64
  177.3 18.0 %while.64 = (s32[]{:T(128)}, bf16[128,128]{1,0:T(8,128)(2,1)S(1)}, f32[15,128,128]{2,1,0:T(8,128)S(1)}, bf16[15,128,128]{2,1,0:T(8,128)(2,1)}, f32[15,128,128]{2...) while((s32[]{:T(128)}, bf16[128,128]{1,0:T(8,128)(2,1)S(1)}, ...), condition=%wide.region_13.14_spmd, body=%wide.region_12.13_spmd.sunk | while | flops 8437763 | bytes 329825 | solution.py:82
  196.0 1.7 collective-permute-start.13
  197.7 1.8 collective-permute-start.14
  199.5 2.0 collective-permute-start.15
  202.6 2.3 collective-permute-start.16
  206.0 6.4 %fusion.45 = f32[2048,128]{0,1:T(8,128)S(1)} fusion(bf16[2048,128]{1,0:T(8,128)(2,1)S(1)} %bitcast.327, bf16[1,1,1,2048,2048]{4,3,2,1,0:T(8,128)(2,1)} %param.27), kind=kOutput, calls=%fused_computation.43 | convolution fusion | flops 1073741824 | bytes 9961472 | tf_op jit(solution)/shard_map/dot_general | solution.py:43
  218.7 1.9 copy.18
  221.7 1.3 multiply_reduce_fusion
  222.9 1.3 copy.19
  224.2 1.5 fusion.48
  225.8 38.7 %all-reduce.1 = (f32[2,128]{1,0:T(2,128)S(1)}, f32[128]{0:T(128)S(1)}) all-reduce(f32[2,128]{1,0:T(2,128)S(1)} %fusion.48, f32[128]{0:T(128)S(1)} %get-tuple-element.426), channel_id=1, replica_groups=mesh['gx'=4,'gy'=4,'gz'=2] {'gx','gy','gz'}, use_global_device_ids=true, to_apply=%region_15.16 | all-reduce | flops 384 | bytes 3072 | tf_op jit(solution)/shard_map/psum | solution.py:134
  264.4 1.3 scatter.16
  266.6 2.8 %multiply_add_fusion = f32[1,1,1,2048,128]{4,3,2,1,0:T(8,128)} fusion(f32[1,1,1,2048,128]{4,3,2,1,0:T(8,128)} %bitcast.326, f32[1,1,1,2048,128]{4,3,2,1,0:T(8,128)} %bitcast.325, bf16[1,1,1,2048,128]{4,3,2,1,0:T(8,128)(2,1)} %param.26, f32[128]{0:T(128)S(1)} %get-tuple-element.413, f32[128]{0:T(128)S(1)} %get-tuple-element.412), kind=kLoop, calls=%fused_computation.56 | loop fusion | flops 1310720 | bytes 3671040 | tf_op jit(solution)/shard_map/add | solution.py:147
  (236 shorter events, 90.8 us)
Async XLA Ops:
  0.6 22.2 %copy-start = (bf16[1,1,1,6,128,128]{5,4,3,2,1,0:T(8,128)(2,1)S(1)}, bf16[1,1,1,6,128,128]{5,4,3,2,1,0:T(8,128)(2,1)}, u32[]{:S(2)}) copy-start(bf16[1,1,1,6,128,128]{5,4,3,2,1,0:T(8,128)(2,1)} %param.28) | copy-start | bytes 589828
  0.6 16.4 %copy-start.8 = (bf16[1,1,1,16,128,128]{5,4,3,2,1,0:T(8,128)(2,1)S(1)}, bf16[1,1,1,16,128,128]{5,4,3,2,1,0:T(8,128)(2,1)}, u32[]{:S(2)}) copy-start(bf16[1,1,1,16,128,128]{5,4,3,2,1,0:T(8,128)(2,1)} %param.29) | copy-start | bytes 1572868
  0.7 22.4 %copy-start.4 = (bf16[1,1,1,2048,128]{4,3,2,1,0:T(8,128)(2,1)S(1)}, bf16[1,1,1,2048,128]{4,3,2,1,0:T(8,128)(2,1)}, u32[]{:S(2)}) copy-start(bf16[1,1,1,2048,128]{4,3,2,1,0:T(8,128)(2,1)} %param.25) | copy-start | bytes 1572868
  1.7 16.9 %collective-permute-start = (bf16[1,2,128,128]{3,2,1,0:T(8,128)(2,1)S(1)}, bf16[1,2,128,128]{3,2,1,0:T(8,128)(2,1)S(1)}, u32[]{:S(2)}, u32[]{:S(2)}) collective-permute-start(bf16[1,2,128,128]{3,2,1,0:T(8,128)(2,1)S(1)} %bitcast.342), channel_id=1, source_target_pairs={{0,8},{8,16},{16,24},{24,0},{1,9},{9,17},{17,25},{25,1},{2,10},{10... | collective-permute-start | bytes 196616 | tf_op jit(solution)/shard_map/ppermute | solution.py:24
  2.2 16.6 %collective-permute-start.1 = (bf16[1,2,128,128]{3,2,1,0:T(8,128)(2,1)S(1)}, bf16[1,2,128,128]{3,2,1,0:T(8,128)(2,1)S(1)}, u32[]{:S(2)}, u32[]{:S(2)}) collective-permute-start(bf16[1,2,128,128]{3,2,1,0:T(8,128)(2,1)S(1)} %bitcast.343), channel_id=1, source_target_pairs={{8,0},{16,8},{24,16},{0,24},{9,1},{17,9},{25,17},{1,25},{10,2},{18... | collective-permute-start | bytes 196616 | tf_op jit(solution)/shard_map/ppermute | solution.py:26
  4.2 14.6 %collective-permute-start.2 = (bf16[1,2,128,128]{3,2,1,0:T(8,128)(2,1)S(1)}, bf16[1,2,128,128]{3,2,1,0:T(8,128)(2,1)S(1)}, u32[]{:S(2)}, u32[]{:S(2)}) collective-permute-start(bf16[1,2,128,128]{3,2,1,0:T(8,128)(2,1)S(1)} %bitcast.340), channel_id=1, source_target_pairs={{0,2},{2,4},{4,6},{6,0},{1,3},{3,5},{5,7},{7,1},{8,10},{10,12},{12... | collective-permute-start | bytes 196616 | tf_op jit(solution)/shard_map/ppermute | solution.py:24
  6.5 12.3 %collective-permute-start.3 = (bf16[1,2,128,128]{3,2,1,0:T(8,128)(2,1)S(1)}, bf16[1,2,128,128]{3,2,1,0:T(8,128)(2,1)S(1)}, u32[]{:S(2)}, u32[]{:S(2)}) collective-permute-start(bf16[1,2,128,128]{3,2,1,0:T(8,128)(2,1)S(1)} %bitcast.341), channel_id=1, source_target_pairs={{2,0},{4,2},{6,4},{0,6},{3,1},{5,3},{7,5},{1,7},{10,8},{12,10},{14... | collective-permute-start | bytes 196616 | tf_op jit(solution)/shard_map/ppermute | solution.py:26
  8.6 10.3 %collective-permute-start.4 = (bf16[1,2,128,128]{3,2,1,0:T(8,128)(2,1)S(1)}, bf16[1,2,128,128]{3,2,1,0:T(8,128)(2,1)S(1)}, u32[]{:S(2)}, u32[]{:S(2)}) collective-permute-start(bf16[1,2,128,128]{3,2,1,0:T(8,128)(2,1)S(1)} %bitcast.338), channel_id=1, source_target_pairs={{0,1},{1,0},{2,3},{3,2},{4,5},{5,4},{6,7},{7,6},{8,9},{9,8},{10,11... | collective-permute-start | bytes 196616 | tf_op jit(solution)/shard_map/ppermute | solution.py:24
  18.6 4.3 %collective-permute-start.5 = (bf16[1,2,128,128]{3,2,1,0:T(8,128)(2,1)S(1)}, bf16[1,2,128,128]{3,2,1,0:T(8,128)(2,1)S(1)}, u32[]{:S(2)}, u32[]{:S(2)}) collective-permute-start(bf16[1,2,128,128]{3,2,1,0:T(8,128)(2,1)S(1)} %bitcast.339), channel_id=1, source_target_pairs={{1,0},{0,1},{3,2},{2,3},{5,4},{4,5},{7,6},{6,7},{9,8},{8,9},{11,10... | collective-permute-start | bytes 196616 | tf_op jit(solution)/shard_map/ppermute | solution.py:26
  99.1 15.0 %collective-permute-start.6 = (bf16[1,2,128,128]{3,2,1,0:T(8,128)(2,1)S(1)}, bf16[1,2,128,128]{3,2,1,0:T(8,128)(2,1)S(1)}, u32[]{:S(2)}, u32[]{:S(2)}) collective-permute-start(bf16[1,2,128,128]{3,2,1,0:T(8,128)(2,1)S(1)} %get-tuple-element.441), channel_id=1, source_target_pairs={{0,8},{8,16},{16,24},{24,0},{1,9},{9,17},{17,25},{25,1},{2,10},{10... | collective-permute-start | bytes 196616 | tf_op jit(solution)/shard_map/ppermute | solution.py:24
  99.1 14.9 %collective-permute-start.7 = (bf16[1,2,128,128]{3,2,1,0:T(8,128)(2,1)S(1)}, bf16[1,2,128,128]{3,2,1,0:T(8,128)(2,1)S(1)}, u32[]{:S(2)}, u32[]{:S(2)}) collective-permute-start(bf16[1,2,128,128]{3,2,1,0:T(8,128)(2,1)S(1)} %get-tuple-element.441), channel_id=1, source_target_pairs={{8,0},{16,8},{24,16},{0,24},{9,1},{17,9},{25,17},{1,25},{10,2},{18... | collective-permute-start | bytes 196616 | tf_op jit(solution)/shard_map/ppermute | solution.py:26
  100.9 13.2 %collective-permute-start.8 = (bf16[1,2,128,128]{3,2,1,0:T(8,128)(2,1)S(1)}, bf16[1,2,128,128]{3,2,1,0:T(8,128)(2,1)S(1)}, u32[]{:S(2)}, u32[]{:S(2)}) collective-permute-start(bf16[1,2,128,128]{3,2,1,0:T(8,128)(2,1)S(1)} %get-tuple-element.440), channel_id=1, source_target_pairs={{0,2},{2,4},{4,6},{6,0},{1,3},{3,5},{5,7},{7,1},{8,10},{10,12},{12... | collective-permute-start | bytes 196616 | tf_op jit(solution)/shard_map/ppermute | solution.py:24
  102.8 11.3 %collective-permute-start.9 = (bf16[1,2,128,128]{3,2,1,0:T(8,128)(2,1)S(1)}, bf16[1,2,128,128]{3,2,1,0:T(8,128)(2,1)S(1)}, u32[]{:S(2)}, u32[]{:S(2)}) collective-permute-start(bf16[1,2,128,128]{3,2,1,0:T(8,128)(2,1)S(1)} %get-tuple-element.440), channel_id=1, source_target_pairs={{2,0},{4,2},{6,4},{0,6},{3,1},{5,3},{7,5},{1,7},{10,8},{12,10},{14... | collective-permute-start | bytes 196616 | tf_op jit(solution)/shard_map/ppermute | solution.py:26
  104.7 14.2 %copy-start.5 = (bf16[1,1,1,2048,128]{4,3,2,1,0:T(8,128)(2,1)S(1)}, bf16[1,1,1,2048,128]{4,3,2,1,0:T(8,128)(2,1)}, u32[]{:S(2)}) copy-start(bf16[1,1,1,2048,128]{4,3,2,1,0:T(8,128)(2,1)} %param.25) | copy-start | bytes 1572868
  104.7 14.2 %copy-start.7 = (f32[1,1280,128]{2,1,0:T(8,128)S(1)}, f32[1,1280,128]{2,1,0:T(8,128)}, u32[]{:S(2)}) copy-start(f32[1,1280,128]{2,1,0:T(8,128)} %get-tuple-element.430) | copy-start | bytes 1966084
  110.7 8.2 %copy-start.3 = (f32[1280,128]{1,0:T(8,128)}, f32[1280,128]{1,0:T(8,128)S(1)}, u32[]{:S(2)}) copy-start(f32[1280,128]{1,0:T(8,128)S(1)} %get-tuple-element.433) | copy-start | bytes 1966084
  110.7 8.6 %copy-start.1 = (f32[1,1280,128]{2,1,0:T(8,128)}, f32[1,1280,128]{2,1,0:T(8,128)S(1)}, u32[]{:S(2)}) copy-start(f32[1,1280,128]{2,1,0:T(8,128)S(1)} %get-tuple-element.432) | copy-start | bytes 1966084
  111.8 5.1 %collective-permute-start.10 = (bf16[1,2,128,128]{3,2,1,0:T(8,128)(2,1)S(1)}, bf16[1,2,128,128]{3,2,1,0:T(8,128)(2,1)S(1)}, u32[]{:S(2)}, u32[]{:S(2)}) collective-permute-start(bf16[1,2,128,128]{3,2,1,0:T(8,128)(2,1)S(1)} %get-tuple-element.439), channel_id=1, source_target_pairs={{0,1},{1,0},{2,3},{3,2},{4,5},{5,4},{6,7},{7,6},{8,9},{9,8},{10,11... | collective-permute-start | bytes 196616 | tf_op jit(solution)/shard_map/ppermute | solution.py:24
  114.1 4.3 %collective-permute-start.11 = (bf16[1,2,128,128]{3,2,1,0:T(8,128)(2,1)S(1)}, bf16[1,2,128,128]{3,2,1,0:T(8,128)(2,1)S(1)}, u32[]{:S(2)}, u32[]{:S(2)}) collective-permute-start(bf16[1,2,128,128]{3,2,1,0:T(8,128)(2,1)S(1)} %get-tuple-element.439), channel_id=1, source_target_pairs={{1,0},{0,1},{3,2},{2,3},{5,4},{4,5},{7,6},{6,7},{9,8},{8,9},{11,10... | collective-permute-start | bytes 196616 | tf_op jit(solution)/shard_map/ppermute | solution.py:26
  157.3 47.5 %copy-start.2 = (f32[1,1280,128]{2,1,0:T(8,128)S(1)}, f32[1,1280,128]{2,1,0:T(8,128)}, u32[]{:S(2)}) copy-start(f32[1,1280,128]{2,1,0:T(8,128)} %copy-done.1) | copy-start | bytes 1966084
  196.0 17.4 %collective-permute-start.12 = (bf16[1,2,128,128]{3,2,1,0:T(8,128)(2,1)}, bf16[1,2,128,128]{3,2,1,0:T(8,128)(2,1)}, u32[]{:S(2)}, u32[]{:S(2)}) collective-permute-start(bf16[1,2,128,128]{3,2,1,0:T(8,128)(2,1)} %get-tuple-element.438), channel_id=1, source_target_pairs={{0,8},{8,16},{16,24},{24,0},{1,9},{9,17},{17,25},{25,1},{2,10},{10... | collective-permute-start | bytes 196616 | tf_op jit(solution)/shard_map/ppermute | solution.py:24
  196.0 18.2 %collective-permute-start.13 = (bf16[1,2,128,128]{3,2,1,0:T(8,128)(2,1)}, bf16[1,2,128,128]{3,2,1,0:T(8,128)(2,1)}, u32[]{:S(2)}, u32[]{:S(2)}) collective-permute-start(bf16[1,2,128,128]{3,2,1,0:T(8,128)(2,1)} %get-tuple-element.438), channel_id=1, source_target_pairs={{8,0},{16,8},{24,16},{0,24},{9,1},{17,9},{25,17},{1,25},{10,2},{18... | collective-permute-start | bytes 196616 | tf_op jit(solution)/shard_map/ppermute | solution.py:26
  197.7 17.3 %collective-permute-start.14 = (bf16[1,2,128,128]{3,2,1,0:T(8,128)(2,1)S(1)}, bf16[1,2,128,128]{3,2,1,0:T(8,128)(2,1)}, u32[]{:S(2)}, u32[]{:S(2)}) collective-permute-start(bf16[1,2,128,128]{3,2,1,0:T(8,128)(2,1)S(1)} %get-tuple-element.437), channel_id=1, source_target_pairs={{0,2},{2,4},{4,6},{6,0},{1,3},{3,5},{5,7},{7,1},{8,10},{10,12},{12... | collective-permute-start | bytes 196616 | tf_op jit(solution)/shard_map/ppermute | solution.py:24
  199.5 16.2 %collective-permute-start.15 = (bf16[1,2,128,128]{3,2,1,0:T(8,128)(2,1)S(1)}, bf16[1,2,128,128]{3,2,1,0:T(8,128)(2,1)}, u32[]{:S(2)}, u32[]{:S(2)}) collective-permute-start(bf16[1,2,128,128]{3,2,1,0:T(8,128)(2,1)S(1)} %get-tuple-element.437), channel_id=1, source_target_pairs={{2,0},{4,2},{6,4},{0,6},{3,1},{5,3},{7,5},{1,7},{10,8},{12,10},{14... | collective-permute-start | bytes 196616 | tf_op jit(solution)/shard_map/ppermute | solution.py:26
  202.6 13.9 %collective-permute-start.16 = (bf16[1,2,128,128]{3,2,1,0:T(8,128)(2,1)S(1)}, bf16[1,2,128,128]{3,2,1,0:T(8,128)(2,1)}, u32[]{:S(2)}, u32[]{:S(2)}) collective-permute-start(bf16[1,2,128,128]{3,2,1,0:T(8,128)(2,1)S(1)} %get-tuple-element.436), channel_id=1, source_target_pairs={{0,1},{1,0},{2,3},{3,2},{4,5},{5,4},{6,7},{7,6},{8,9},{9,8},{10,11... | collective-permute-start | bytes 196616 | tf_op jit(solution)/shard_map/ppermute | solution.py:24
  206.0 18.2 %copy-start.6 = (f32[1,2048,128]{2,1,0:T(8,128)S(1)}, f32[1,2048,128]{2,1,0:T(8,128)}, u32[]{:S(2)}) copy-start(f32[1,2048,128]{2,1,0:T(8,128)} %subtract_divide_fusion.1) | copy-start | bytes 3145732
  212.4 53.5 %copy-start.9 = (f32[3]{0:T(128)S(1)}, f32[3]{0:T(128)}, u32[]{:S(2)}) copy-start(f32[3]{0:T(128)} %constant.255.clone.1) | copy-start | bytes 40
  213.4 4.3 %collective-permute-start.17 = (bf16[1,2,128,128]{3,2,1,0:T(8,128)(2,1)S(1)}, bf16[1,2,128,128]{3,2,1,0:T(8,128)(2,1)S(1)}, u32[]{:S(2)}, u32[]{:S(2)}) collective-permute-start(bf16[1,2,128,128]{3,2,1,0:T(8,128)(2,1)S(1)} %get-tuple-element.436), channel_id=1, source_target_pairs={{1,0},{0,1},{3,2},{2,3},{5,4},{4,5},{7,6},{6,7},{9,8},{8,9},{11,10... | collective-permute-start | bytes 196616 | tf_op jit(solution)/shard_map/ppermute | solution.py:26
where the time goes:
time: 273 us; the launch traced here: 269 us
  blocking collectives  115 us (42%)
  matrix products  86.2 us (32%)
  starting transfers between devices  24.7 us (9%)
  local copies, waits for them, and re-layouts  16.3 us (6%)
  other arithmetic  16.3 us (6%)
  waiting for transfers between devices  8.5 us (3%)
    psum x2, blocking collectives, body(): lax.psum((own_products, jnp.sum(mapped * mapped, axis=0)), ('gx', 'gy', '...  76.8 us
    psum x1, blocking collectives, body(): lax.psum(jnp.sum(residual * residual, axis=0), ('gx', 'gy', 'gz')) + epsilon  37.7 us
    dot_general x30, matrix products, backward(): jnp.dot(diag_block, inner.astype(jnp.bfloat16), preferred_element_type=jn...  34.9 us
    dot_general x30, matrix products, forward(): jnp.dot(lower_block, previous.astype(jnp.bfloat16), preferred_element_typ...  30.1 us
    dot_general x3, matrix products, operate(): own_part = jnp.dot(schur_block, values, preferred_element_type=jnp.float32)  18.1 us
    ppermute x9, starting transfers between devices, with_halo(): lax.ppermute(tail, axis, [(i, (i + 1) % count) for i in range(count)])  13 us
    ppermute x9, starting transfers between devices, with_halo(): lax.ppermute(head, axis, [((i + 1) % count, i) for i in range(count)])  11.7 us
    ppermute x9, waiting for transfers between devices, with_halo(): lax.ppermute(head, axis, [((i + 1) % count, i) for i in range(count)])  5.72 us
  transfers between devices with their start and end apart: 18, of which 4 were waited for; matrix products, arithmetic and copies ran while one was open for 11% of the time, Pallas kernels for 0%

commit v1 on v0

v1 whole, which is shorter than its diff:
```python
import functools

import jax
import jax.numpy as jnp
from jax import lax
from jax.experimental import pallas as pl
from jax.experimental.pallas import tpu as pltpu
from jax.sharding import PartitionSpec as P

AXES = ("gx", "gy", "gz")
MESH = pl.DeviceIdType.MESH
EPS = 1e-06
GROUP = 4
bf16 = jnp.bfloat16
f32 = jnp.float32


def dot(a, b):
    return jnp.dot(a, b, preferred_element_type=f32)


def split(v):
    hi = v.astype(bf16)
    lo = (v - hi.astype(f32)).astype(bf16)
    return jnp.concatenate([hi, lo], axis=1)


def fold(y):
    r = y.shape[1] // 2
    return y[:, :r] + y[:, r:]


def colsum(v):
    return jnp.sum(v, axis=0, keepdims=True)


def least_squares(h, start_norm):
    t00 = jnp.sqrt(h[0][0] * h[0][0] + h[1][0] * h[1][0])
    q0 = [h[0][0] / t00, h[1][0] / t00]
    t01 = q0[0] * h[0][1] + q0[1] * h[1][1]
    v1 = [h[0][1] - t01 * q0[0], h[1][1] - t01 * q0[1], h[2][1]]
    t11 = jnp.sqrt(v1[0] * v1[0] + v1[1] * v1[1] + v1[2] * v1[2])
    c1 = start_norm * (v1[0] / t11) / t11
    c0 = (start_norm * q0[0] - t01 * c1) / t00
    e0 = start_norm - h[0][0] * c0 - h[0][1] * c1
    e1 = h[1][0] * c0 + h[1][1] * c1
    e2 = h[2][1] * c1
    return c0, c1, jnp.sqrt(e0 * e0 + e1 * e1 + e2 * e2) / start_norm


def kernel(
    sizes, phases, b_hbm, x_hbm, s_hbm, c_hbm, d_hbm, l_hbm, u_hbm,
    d1_hbm, d2_hbm, coef_ref, ratio_ref,
    s_v, c_v, d_v, l_v, u_v, b_v, x_v,
    t_v, cf_v, e_v, z_v, cb_v,
    r0_v, m1_v, w_v, wcat_v, d1_v, d2_v, xcat_v,
    nb0_v, nb1_v, nb2_v, sum_bufs,
    s_sem, in_sem, out_sem, send_sem, recv_sem, sum_send, sum_recv,
):
    nb, blk = d_v.shape[0], d_v.shape[1]
    rhs = b_v.shape[1]
    unknowns = b_v.shape[0]
    faces = c_v.shape[0]
    fr = faces * blk
    groups = nb // GROUP
    chunks = s_sem.shape[0]
    rows = unknowns // chunks
    me = {a: lax.axis_index(a) for a in AXES}

    loads = [
        pltpu.make_async_copy(l_hbm, l_v, in_sem.at[0]),
        pltpu.make_async_copy(x_hbm, x_v, in_sem.at[1]),
        pltpu.make_async_copy(u_hbm, u_v, in_sem.at[2]),
        pltpu.make_async_copy(d_hbm, d_v, in_sem.at[3]),
    ]
    s_loads = [
        pltpu.make_async_copy(
            s_hbm.at[pl.ds(i * rows, rows)], s_v.at[pl.ds(i * rows, rows)], s_sem.at[i]
        )
        for i in range(chunks)
    ]
    late = [
        pltpu.make_async_copy(b_hbm, b_v, in_sem.at[4]),
        pltpu.make_async_copy(c_hbm, c_v, in_sem.at[5]),
    ]
    for c in loads + s_loads + late:
        c.start()

    def peer_of(names, k):
        index, count = 0, 1
        for a in names:
            index = index * sizes[a] + me[a]
            count = count * sizes[a]
        other = lax.rem(index + k, count)
        ids, left = {}, other
        for a in reversed(names):
            ids[a] = lax.rem(left, sizes[a])
            left = left // sizes[a]
        return index, other, count, ids

    barrier = pltpu.get_barrier_semaphore()
    greeted = 0
    for names in phases:
        count = 1
        for a in names:
            count *= sizes[a]
        for k in range(1, count):
            pl.semaphore_signal(
                barrier, inc=1, device_id=peer_of(names, k)[3], device_id_type=MESH
            )
            greeted += 1

    def halo(src, dst, stage):
        copies = []
        for f in range(faces):
            a = AXES[f // 2]
            step = 1 if f % 2 else sizes[a] - 1
            copies.append(
                pltpu.make_async_remote_copy(
                    src_ref=src.at[pl.ds(f * blk, blk)],
                    dst_ref=dst.at[f ^ 1],
                    send_sem=send_sem.at[stage, f],
                    recv_sem=recv_sem.at[stage, f ^ 1],
                    device_id={a: lax.rem(me[a] + step, sizes[a])},
                    device_id_type=MESH,
                )
            )
        for c in copies:
            c.start()
        return copies

    loads[0].wait()
    for g in range(groups):
        a = g * GROUP
        for i in range(1, GROUP):
            t_v[g, pl.ds(i * blk, blk), pl.ds((i - 1) * blk, blk)] = -l_v[a + i - 1]
        for i in range(2, GROUP):
            width = (i - 1) * blk
            before = t_v[g, pl.ds((i - 1) * blk, blk), pl.ds(0, width)]
            t_v[g, pl.ds(i * blk, blk), pl.ds(0, width)] = (
                -dot(l_v[a + i - 1], before)
            ).astype(bf16)
        if g > 0:
            carry = -l_v[a - 1]
            cf_v[g, pl.ds(0, blk)] = carry
            for i in range(1, GROUP):
                carry = (-dot(l_v[a + i - 1], carry)).astype(bf16)
                cf_v[g, pl.ds(i * blk, blk)] = carry

    pl.semaphore_wait(barrier, greeted)
    first = halo(x_hbm, nb0_v, 0)

    loads[2].wait()
    loads[3].wait()
    for k in range(nb - 1):
        e_v[k] = (-dot(d_v[k], u_v[k])).astype(bf16)
    for g in range(groups):
        a = g * GROUP
        for i in range(GROUP - 1, -1, -1):
            z_v[g, pl.ds(i * blk, blk), pl.ds(i * blk, blk)] = d_v[a + i]
            if i < GROUP - 1:
                width = (GROUP - 1 - i) * blk
                after = z_v[g, pl.ds((i + 1) * blk, blk), pl.ds((i + 1) * blk, width)]
                z_v[g, pl.ds(i * blk, blk), pl.ds((i + 1) * blk, width)] = dot(
                    e_v[a + i], after
                ).astype(bf16)
        if g < groups - 1:
            carry = e_v[a + GROUP - 1]
            cb_v[g, pl.ds((GROUP - 1) * blk, blk)] = carry
            for i in range(GROUP - 2, -1, -1):
                carry = dot(e_v[a + i], carry).astype(bf16)
                cb_v[g, pl.ds(i * blk, blk)] = carry

    loads[1].wait()
    for i in range(chunks):
        s_loads[i].wait()
        r0_v[pl.ds(i * rows, rows)] = -dot(s_v[pl.ds(i * rows, rows)], x_v[...])
    late[0].wait()
    late[1].wait()
    g00 = jnp.zeros((1, rhs), f32)
    for i in range(nb - 1, -1, -1):
        here = pl.ds(i * blk, blk)
        r = r0_v[here] + b_v[here].astype(f32)
        if i < faces:
            first[i ^ 1].wait_recv()
            r = r - dot(c_v[i], nb0_v[i])
        r0_v[here] = r
        g00 = g00 + colsum(r * r)

    def precondition(v_v, z_out):
        gs = GROUP * blk
        last = None
        for g in range(groups):
            rows_g = pl.ds(g * gs, gs)
            cat = split(v_v[rows_g])
            parts = [v_v[pl.ds(g * gs, blk)]]
            for i in range(1, GROUP):
                parts.append(
                    v_v[pl.ds(g * gs + i * blk, blk)]
                    + fold(dot(t_v[g, pl.ds(i * blk, blk), pl.ds(0, i * blk)], cat[: i * blk]))
                )
            w_v[rows_g] = jnp.concatenate(parts, axis=0)
        for g in range(groups):
            rows_g = pl.ds(g * gs, gs)
            w = w_v[rows_g]
            if g > 0:
                w = w + fold(dot(cf_v[g], last))
            cat = split(w)
            wcat_v[rows_g] = cat
            last = cat[gs - blk :]
        for g in range(groups):
            for i in range(GROUP):
                here = pl.ds(g * gs + i * blk, blk)
                rest = (GROUP - i) * blk
                z_out[here] = fold(
                    dot(
                        z_v[g, pl.ds(i * blk, blk), pl.ds(i * blk, rest)],
                        wcat_v[pl.ds(g * gs + i * blk, rest)],
                    )
                )
        for g in range(groups - 2, -1, -1):
            head = split(z_out[pl.ds((g + 1) * gs, blk)])
            rows_g = pl.ds(g * gs, gs)
            z_out[rows_g] = z_out[rows_g] + fold(dot(cb_v[g], head))

    precondition(r0_v, d1_v)
    for i in range(nb):
        here = pl.ds(i * blk, blk)
        xcat_v[0, here] = split(d1_v[here])
    second = halo(xcat_v.at[0], nb1_v, 1)
    d1_out = pltpu.make_async_copy(d1_v, d1_hbm, out_sem.at[0])
    d1_out.start()
    m1_v[pl.ds(fr, unknowns - fr)] = (
        fold(dot(s_v[pl.ds(fr, unknowns - fr)], xcat_v[0])) - r0_v[pl.ds(fr, unknowns - fr)]
    )
    m1_v[pl.ds(0, fr)] = fold(dot(s_v[pl.ds(0, fr)], xcat_v[0])) - r0_v[pl.ds(0, fr)]
    g01 = jnp.zeros((1, rhs), f32)
    g11 = jnp.zeros((1, rhs), f32)
    for i in range(nb - 1, -1, -1):
        here = pl.ds(i * blk, blk)
        m = m1_v[here]
        if i < faces:
            second[i ^ 1].wait_recv()
            m = m + fold(dot(c_v[i], nb1_v[i]))
            m1_v[here] = m
        g01 = g01 + colsum(m * r0_v[here])
        g11 = g11 + colsum(m * m)

    precondition(m1_v, d2_v)
    for i in range(nb):
        here = pl.ds(i * blk, blk)
        x_v[here] = d2_v[here].astype(bf16)
    third = halo(x_v, nb2_v, 2)
    d2_out = pltpu.make_async_copy(d2_v, d2_hbm, out_sem.at[1])
    d2_out.start()
    w_v[pl.ds(fr, unknowns - fr)] = dot(s_v[pl.ds(fr, unknowns - fr)], x_v[...])
    w_v[pl.ds(0, fr)] = dot(s_v[pl.ds(0, fr)], x_v[...])
    g02 = jnp.zeros((1, rhs), f32)
    g12 = jnp.zeros((1, rhs), f32)
    g22 = jnp.zeros((1, rhs), f32)
    for i in range(nb - 1, -1, -1):
        here = pl.ds(i * blk, blk)
        m = w_v[here]
        if i < faces:
            third[i ^ 1].wait_recv()
            m = m + dot(c_v[i], nb2_v[i])
        g02 = g02 + colsum(m * r0_v[here])
        g12 = g12 + colsum(m * m1_v[here])
        g22 = g22 + colsum(m * m)

    zero = jnp.zeros((1, rhs), f32)
    total = jnp.concatenate([g00, g01, g11, g02, g12, g22, zero, zero], axis=0)
    base = 0
    for p, names in enumerate(phases):
        buf = sum_bufs[p]
        index, _, count, _ = peer_of(names, 0)
        buf[index] = total
        copies = []
        for k in range(1, count):
            ids = peer_of(names, k)[3]
            copies.append(
                pltpu.make_async_remote_copy(
                    src_ref=buf.at[index],
                    dst_ref=buf.at[index],
                    send_sem=sum_send.at[base + k],
                    recv_sem=sum_recv.at[base + index],
                    device_id=ids,
                    device_id_type=MESH,
                )
            )
        for c in copies:
            c.start()
        for k in range(1, count):
            other = peer_of(names, k)[1]
            pltpu.make_async_copy(
                buf.at[other], buf.at[other], sum_recv.at[base + other]
            ).wait()
        total = buf[0]
        for k in range(1, count):
            total = total + buf[k]
        for c in copies:
            c.wait_send()
        base += count

    g00, g01, g11, g02, g12, g22 = [total[i : i + 1] for i in range(6)]
    b2 = g00 + EPS
    start = jnp.sqrt(b2)
    h00 = (g01 + g00) / b2
    de = h00 - 1.0
    n1 = (g11 - 2.0 * de * g01 + de * de * g00) / b2
    h10 = jnp.sqrt(jnp.maximum(n1, 0.0) + EPS)
    s2 = start * h10
    r0q = g02 - de * (g01 + g00)
    m1q = g12 - de * (g11 + g01)
    h01 = r0q / (start * s2)
    h11 = (m1q - de * r0q) / (s2 * s2)
    qq = (
        g22 - 2.0 * de * (g12 + g02) + de * de * (g11 + 2.0 * g01 + g00)
    ) / (s2 * s2)
    k00 = g00 / b2
    k11 = n1 / (h10 * h10)
    k01 = (g01 - de * g00) / (start * s2)
    n2 = qq - 2.0 * (h01 * h01 + h11 * h11) + h01 * h01 * k00 + h11 * h11 * k11
    n2 = n2 + 2.0 * h01 * h11 * k01
    h21 = jnp.sqrt(jnp.maximum(n2, 0.0) + EPS)
    c0, c1, ratio = least_squares([[h00, h01], [h10, h11], [zero, h21]], start)
    a2 = c1 / s2
    coef_ref[...] = jnp.concatenate([c0 / start - de * a2, a2], axis=0)
    ratio_ref[...] = ratio
    for c in first + second + third:
        c.wait_send()
    d1_out.wait()
    d2_out.wait()


def body(sizes, loads, start_guess, schur, coupling, diag_inverse, lower, upper):
    b, x, s, c, d, l, u = [
        v.reshape(v.shape[3:])
        for v in (loads, start_guess, schur, coupling, diag_inverse, lower, upper)
    ]
    n, r = b.shape
    nb, blk = d.shape[:2]
    faces = c.shape[0]
    groups = nb // GROUP
    gs = GROUP * blk
    chunks = 4
    phases = (("gx",), ("gy", "gz"))
    if sizes["gy"] * sizes["gz"] > 32:
        phases = (("gx",), ("gy",), ("gz",))
    counts = []
    for names in phases:
        count = 1
        for a in names:
            count *= sizes[a]
        counts.append(count)
    any_spec = pl.BlockSpec(memory_space=pl.ANY)
    vmem = pl.BlockSpec(memory_space=pltpu.VMEM)
    d1, d2, coef, ratio = pl.pallas_call(
        functools.partial(kernel, sizes, phases),
        out_shape=(
            jax.ShapeDtypeStruct((n, r), f32),
            jax.ShapeDtypeStruct((n, r), f32),
            jax.ShapeDtypeStruct((2, r), f32),
            jax.ShapeDtypeStruct((1, r), f32),
        ),
        in_specs=[any_spec] * 7,
        out_specs=(any_spec, any_spec, vmem, vmem),
        scratch_shapes=[
            pltpu.VMEM(s.shape, bf16),
            pltpu.VMEM(c.shape, bf16),
            pltpu.VMEM(d.shape, bf16),
            pltpu.VMEM(l.shape, bf16),
            pltpu.VMEM(u.shape, bf16),
            pltpu.VMEM((n, r), bf16),
            pltpu.VMEM((n, r), bf16),
            pltpu.VMEM((groups, gs, gs), bf16),
            pltpu.VMEM((groups, gs, blk), bf16),
            pltpu.VMEM((nb - 1, blk, blk), bf16),
            pltpu.VMEM((groups, gs, gs), bf16),
            pltpu.VMEM((groups, gs, blk), bf16),
            pltpu.VMEM((n, r), f32),
            pltpu.VMEM((n, r), f32),
            pltpu.VMEM((n, r), f32),
            pltpu.VMEM((n, 2 * r), bf16),
            pltpu.VMEM((n, r), f32),
            pltpu.VMEM((n, r), f32),
            pltpu.VMEM((1, n, 2 * r), bf16),
            pltpu.VMEM((faces, blk, r), bf16),
            pltpu.VMEM((faces, blk, 2 * r), bf16),
            pltpu.VMEM((faces, blk, r), bf16),
            [pltpu.VMEM((count, 8, r), f32) for count in counts],
            pltpu.SemaphoreType.DMA((chunks,)),
            pltpu.SemaphoreType.DMA((6,)),
            pltpu.SemaphoreType.DMA((2,)),
            pltpu.SemaphoreType.DMA((3, faces)),
            pltpu.SemaphoreType.DMA((3, faces)),
            pltpu.SemaphoreType.DMA((sum(counts),)),
            pltpu.SemaphoreType.DMA((sum(counts),)),
        ],
        compiler_params=pltpu.CompilerParams(collective_id=0, has_side_effects=True),
    )(b, x, s, c, d, l, u)
    out = x.astype(f32) + coef[0:1] * d1 + coef[1:2] * d2
    return out[None, None, None], ratio.reshape(r)


def solution(mesh):
    sizes = {a: mesh.shape[a] for a in AXES}
    deep = P("gx", "gy", "gz", None, None, None)
    flat = P("gx", "gy", "gz", None, None)
    return jax.shard_map(
        functools.partial(body, sizes),
        mesh=mesh,
        in_specs=(flat, flat, flat, deep, deep, deep, deep),
        out_specs=(flat, P()),
        check_vma=False,
    )
```

time: 273 us -> 41.9 us (0.15); the launches traced: 269 us -> 41.7 us
  blocking collectives: 115 us -> 0 us
  matrix products: 86.2 us -> 0 us
  Pallas kernels: 0 us -> 36.5 us
  starting transfers between devices: 24.7 us -> 0 us
  local copies, waits for them, and re-layouts: 16.3 us -> 1.86 us
  other arithmetic: 16.3 us -> 2.68 us
  waiting for transfers between devices: 8.5 us -> 0 us
    psum x3 -> x0, blocking collectives: 115 us -> none  [the longest x2 76.8 us: body(): lax.psum((own_products, jnp.sum(mapped * mapped, axis=0)), ('gx', 'gy', '...]
    dot_general x68 -> x0, matrix products: 86.2 us -> none  [the longest x30 34.9 us: backward(): jnp.dot(diag_block, inner.astype(jnp.bfloat16), preferred_element_type=jn...]
    pallas_call x0 -> x1, Pallas kernels: none -> 36.5 us  [body(): pl.pallas_call(functools.partial(kernel, sizes, phases), out_shape=(jax.S...]
    ppermute x18 -> x0, starting transfers between devices: 24.7 us -> none  [the longest x9 13 us: with_halo(): lax.ppermute(tail, axis, [(i, (i + 1) % count) for i in range(count)])]
    ppermute x18 -> x0, waiting for transfers between devices: 8.5 us -> none  [the longest x9 5.72 us: with_halo(): lax.ppermute(head, axis, [((i + 1) % count, i) for i in range(count)])]
    slice x6 -> x0, local copies, waits for them, and re-layouts: 4.75 us -> none  [the longest x2 2.02 us: precondition(): carried, remaining = lax.scan(forward, blocks[0], (blocks[1:], lower_one))]
    concatenate x4 -> x0, other arithmetic: 4.2 us -> none  [the longest x2 2.16 us: precondition(): return jnp.concatenate([earlier, final_block[None]], axis=0).reshape(U, R)]
    div x6 -> x0, other arithmetic: 4.12 us -> none  [the longest x2 2.42 us: body(): krylov.append(mapped / length)]
  transfers between devices with their start and end apart: 18 -> 0, of which waited for: 4 -> 0; matrix products, arithmetic and copies ran while one was open for 11% -> 0% of each run, Pallas kernels for 0% -> 0%
where the time goes in v1:
time: 41.9 us; the launch traced here: 41.7 us
  Pallas kernels  36.5 us (87%)
  other arithmetic  2.68 us (6%)
  local copies, waits for them, and re-layouts  1.86 us (4%)
  between operations  0.65 us (2%)
    pallas_call x1, Pallas kernels, body(): pl.pallas_call(functools.partial(kernel, sizes, phases), out_shape=(jax.S...  36.5 us
    broadcast_in_dim x1, other arithmetic, body(): return (out[None, None, None], ratio.reshape(r))  2.68 us
    unnamed x3, local copies, waits for them, and re-layouts  1.17 us

profile of v1, /device:TPU:0, one launch (start us, length us, event | category | flops | bytes accessed | tf_op | source)
XLA Modules:
  0.0 41.7 jit_solution(3006072739985715647)
XLA Ops:
  0.6 0.0 copy-start
  0.6 36.5 %shard_map.86 = (f32[2048,128]{1,0:T(8,128)}, f32[2048,128]{1,0:T(8,128)}, f32[2,128]{1,0:T(2,128)}, f32[1,128]{1,0:T(1,128)}) custom-call(bf16[2048,128]{1,0:T(8,128)(2,1)} %bitcast.17, bf16[2048,128]{1,0:T(8,128)(2,1)} %bitcast.16, bf16[2048,2048]{1,0:T(8,128)(2,1)} %bitcast.15, bf16[6,128,128]{2,1,0:T(8,128)(2,1)} %bitcast.21, ...), custom_call_target="tpu_custom_call" | custom-call | tf_op jit(solution)/shard_map/pallas_call | solution.py:358
  37.2 0.7 %slice_bitcast_fusion.1 = (f32[128]{0:T(128)S(1)}, f32[128]{0:T(128)S(1)}) fusion(f32[2,128]{1,0:T(2,128)} %get-tuple-element.6), kind=kLoop, calls=%fused_computation.2 | loop fusion | bytes 2048 | tf_op jit(solution)/shard_map/mul | solution.py:402
  37.9 0.0 copy-done
  37.9 2.7 %add_bitcast_fusion = f32[1,1,1,2048,128]{4,3,2,1,0:T(8,128)} fusion(f32[2048,128]{1,0:T(8,128)} %get-tuple-element.8, f32[2048,128]{1,0:T(8,128)} %get-tuple-element.7, f32[128]{0:T(128)S(1)} %get-tuple-element.11, f32[128]{0:T(128)S(1)} %get-tuple-element.10, bf16[1,1,1,2048,128]{4,3,2,1,0:T(8,128)(2,1)S(1)} %copy-done), kind=kLoop, calls=%fused_computation | loop fusion | flops 1310720 | bytes 3671040 | tf_op jit(solution)/shard_map/broadcast_in_dim | solution.py:403
  40.6 1.2 %copy.10 = f32[128]{0:T(128)} copy(f32[128]{0:T(128)} %bitcast.22) | data formatting | bytes 1024
Async XLA Ops:
  0.6 37.2 %copy-start = (bf16[1,1,1,2048,128]{4,3,2,1,0:T(8,128)(2,1)S(1)}, bf16[1,1,1,2048,128]{4,3,2,1,0:T(8,128)(2,1)}, u32[]{:S(2)}) copy-start(bf16[1,1,1,2048,128]{4,3,2,1,0:T(8,128)(2,1)} %param.8) | copy-start | bytes 1572868

commit v2 on v1

v2 whole, which is shorter than its diff:
```python
import functools
import itertools
import math

import jax
import jax.numpy as jnp
from jax import lax
from jax.experimental import pallas as pl
from jax.experimental.pallas import tpu as pltpu
from jax.sharding import PartitionSpec as P

AXES = ("gx", "gy", "gz")
MESH = pl.DeviceIdType.MESH
EPS = 1e-06
GROUP = 4
bf16 = jnp.bfloat16
f32 = jnp.float32


def dot(a, b):
    return jnp.dot(a, b, preferred_element_type=f32)


def split(v):
    hi = v.astype(bf16)
    lo = (v - hi.astype(f32)).astype(bf16)
    return jnp.concatenate([hi, lo], axis=1)


def fold(y):
    r = y.shape[1] // 2
    return y[:, :r] + y[:, r:]


def colsum(v):
    return jnp.sum(v, axis=0, keepdims=True)


def least_squares(h, start_norm):
    t00 = jnp.sqrt(h[0][0] * h[0][0] + h[1][0] * h[1][0])
    q0 = [h[0][0] / t00, h[1][0] / t00]
    t01 = q0[0] * h[0][1] + q0[1] * h[1][1]
    v1 = [h[0][1] - t01 * q0[0], h[1][1] - t01 * q0[1], h[2][1]]
    t11 = jnp.sqrt(v1[0] * v1[0] + v1[1] * v1[1] + v1[2] * v1[2])
    c1 = start_norm * (v1[0] / t11) / t11
    c0 = (start_norm * q0[0] - t01 * c1) / t00
    e0 = start_norm - h[0][0] * c0 - h[0][1] * c1
    e1 = h[1][0] * c0 + h[1][1] * c1
    e2 = h[2][1] * c1
    return c0, c1, jnp.sqrt(e0 * e0 + e1 * e1 + e2 * e2) / start_norm


def kernel(
    sizes, phases, b_hbm, x_hbm, s_hbm, c_hbm, d_hbm, l_hbm, u_hbm,
    x_v, d1_v, d2_v, coef_ref, ratio_ref,
    s_v, c_v, d_v, l_v, u_v, b_v, xd_v,
    t_v, cf_v, e_v, z_v, cb_v,
    r0_v, m1_v, w_v, wcat_v, xcat_v, face_v,
    nb0_v, nb1_v, nb2_v, sum_bufs,
    s_sem, in_sem, send_sem, recv_sem, sum_send, sum_recv,
):
    nb, blk = d_v.shape[0], d_v.shape[1]
    rhs = b_v.shape[1]
    unknowns = b_v.shape[0]
    faces = c_v.shape[0]
    fr = faces * blk
    groups = nb // GROUP
    chunks = s_sem.shape[0]
    rows = unknowns // chunks
    me = {a: lax.axis_index(a) for a in AXES}

    loads = [
        pltpu.make_async_copy(l_hbm, l_v, in_sem.at[0]),
        pltpu.make_async_copy(x_hbm, x_v, in_sem.at[1]),
        pltpu.make_async_copy(u_hbm, u_v, in_sem.at[2]),
        pltpu.make_async_copy(d_hbm, d_v, in_sem.at[3]),
    ]
    s_loads = [
        pltpu.make_async_copy(
            s_hbm.at[pl.ds(i * rows, rows)], s_v.at[pl.ds(i * rows, rows)], s_sem.at[i]
        )
        for i in range(chunks)
    ]
    late = [
        pltpu.make_async_copy(b_hbm, b_v, in_sem.at[4]),
        pltpu.make_async_copy(c_hbm, c_v, in_sem.at[5]),
    ]
    for c in loads + s_loads + late:
        c.start()

    away = {
        a: [me[a]] + [lax.rem(me[a] + k, sizes[a]) for k in range(1, sizes[a])] for a in AXES
    }

    def place(names, ids):
        index = 0
        for a in names:
            index = index * sizes[a] + ids[a]
        return index

    def peers(names):
        steps = itertools.product(*[range(sizes[a]) for a in names])
        return [
            {a: away[a][k] for a, k in zip(names, step)} for step in steps if any(step)
        ]

    barrier = pltpu.get_barrier_semaphore()
    greeted = 0
    for names in phases:
        for ids in peers(names):
            pl.semaphore_signal(barrier, inc=1, device_id=ids, device_id_type=MESH)
            greeted += 1

    def face_copy(src, dst, stage, f):
        a = AXES[f // 2]
        step = 1 if f % 2 else sizes[a] - 1
        return pltpu.make_async_remote_copy(
            src_ref=src,
            dst_ref=dst.at[f ^ 1],
            send_sem=send_sem.at[stage, f],
            recv_sem=recv_sem.at[stage, f ^ 1],
            device_id={a: lax.rem(me[a] + step, sizes[a])},
            device_id_type=MESH,
        )

    loads[0].wait()
    for g in range(groups):
        a = g * GROUP
        for i in range(1, GROUP):
            t_v[g, pl.ds(i * blk, blk), pl.ds((i - 1) * blk, blk)] = -l_v[a + i - 1]
        for i in range(2, GROUP):
            width = (i - 1) * blk
            before = t_v[g, pl.ds((i - 1) * blk, blk), pl.ds(0, width)]
            t_v[g, pl.ds(i * blk, blk), pl.ds(0, width)] = (
                -dot(l_v[a + i - 1], before)
            ).astype(bf16)
        if g > 0:
            carry = -l_v[a - 1]
            cf_v[g, pl.ds(0, blk)] = carry
            for i in range(1, GROUP):
                carry = (-dot(l_v[a + i - 1], carry)).astype(bf16)
                cf_v[g, pl.ds(i * blk, blk)] = carry

    loads[2].wait()
    loads[3].wait()
    for k in range(nb - 1):
        e_v[k] = (-dot(d_v[k], u_v[k])).astype(bf16)

    pl.semaphore_wait(barrier, greeted)
    first = [
        face_copy(x_hbm.at[pl.ds(f * blk, blk)], nb0_v, 0, f) for f in range(faces)
    ]
    for c in reversed(first):
        c.start()

    for g in range(groups):
        a = g * GROUP
        for i in range(GROUP - 1, -1, -1):
            z_v[g, pl.ds(i * blk, blk), pl.ds(i * blk, blk)] = d_v[a + i]
            if i < GROUP - 1:
                width = (GROUP - 1 - i) * blk
                after = z_v[g, pl.ds((i + 1) * blk, blk), pl.ds((i + 1) * blk, width)]
                z_v[g, pl.ds(i * blk, blk), pl.ds((i + 1) * blk, width)] = dot(
                    e_v[a + i], after
                ).astype(bf16)
        if g < groups - 1:
            carry = e_v[a + GROUP - 1]
            cb_v[g, pl.ds((GROUP - 1) * blk, blk)] = carry
            for i in range(GROUP - 2, -1, -1):
                carry = dot(e_v[a + i], carry).astype(bf16)
                cb_v[g, pl.ds(i * blk, blk)] = carry

    loads[1].wait()
    for i in range(chunks):
        s_loads[i].wait()
        r0_v[pl.ds(i * rows, rows)] = -dot(s_v[pl.ds(i * rows, rows)], x_v[...])
    late[0].wait()
    late[1].wait()
    g00 = jnp.zeros((1, rhs), f32)
    for i in range(nb - 1, -1, -1):
        here = pl.ds(i * blk, blk)
        r = r0_v[here] + b_v[here].astype(f32)
        if i < faces:
            first[i ^ 1].wait_recv()
            r = r - dot(c_v[i], nb0_v[i])
        r0_v[here] = r
        g00 = g00 + colsum(r * r)

    gs = GROUP * blk

    def sweep_local(v_v, g):
        cat = split(v_v[pl.ds(g * gs, gs)])
        for i in range(GROUP):
            here = pl.ds(g * gs + i * blk, blk)
            w = v_v[here]
            if i > 0:
                w = w + fold(dot(t_v[g, pl.ds(i * blk, blk), pl.ds(0, i * blk)], cat[: i * blk]))
            w_v[here] = w

    def sweep_rest(z_out, finish):
        last = None
        for g in range(groups):
            rows_g = pl.ds(g * gs, gs)
            w = w_v[rows_g]
            if g > 0:
                w = w + fold(dot(cf_v[g], last))
            cat = split(w)
            wcat_v[rows_g] = cat
            last = cat[gs - blk :]
        head = None
        for g in range(groups - 1, -1, -1):
            for i in range(GROUP):
                b = g * GROUP + i
                rest = (GROUP - i) * blk
                z = fold(
                    dot(
                        z_v[g, pl.ds(i * blk, blk), pl.ds(i * blk, rest)],
                        wcat_v[pl.ds(b * blk, rest)],
                    )
                )
                if head is not None:
                    z = z + fold(dot(cb_v[g, pl.ds(i * blk, blk)], head))
                z_out[pl.ds(b * blk, blk)] = z
                finish(b, z)
                if i == 0:
                    following = split(z)
            head = following

    outside = pl.ds(fr, unknowns - fr)
    inside = pl.ds(0, fr)
    clear = -(-faces // GROUP)

    for g in range(groups):
        sweep_local(r0_v, g)
    second = {}

    def finish_first(b, z):
        cat = split(z)
        xcat_v[pl.ds(b * blk, blk)] = cat
        if b < faces:
            face_v[b] = cat[:, :rhs]
            second[b] = face_copy(face_v.at[b], nb1_v, 1, b)
            second[b].start()

    sweep_rest(d1_v, finish_first)
    g01 = jnp.zeros((1, rhs), f32)
    g11 = jnp.zeros((1, rhs), f32)
    m1_v[outside] = fold(dot(s_v[outside], xcat_v[...])) - r0_v[outside]
    for i in range(faces, nb):
        here = pl.ds(i * blk, blk)
        m = m1_v[here]
        g01 = g01 + colsum(m * r0_v[here])
        g11 = g11 + colsum(m * m)
    for g in range(clear, groups):
        sweep_local(m1_v, g)
    m1_v[inside] = fold(dot(s_v[inside], xcat_v[...])) - r0_v[inside]
    for i in range(faces - 1, -1, -1):
        here = pl.ds(i * blk, blk)
        second[i ^ 1].wait_recv()
        m = m1_v[here] + dot(c_v[i], nb1_v[i])
        m1_v[here] = m
        g01 = g01 + colsum(m * r0_v[here])
        g11 = g11 + colsum(m * m)

    starts = [0]
    for names in phases:
        starts.append(starts[-1] + math.prod(sizes[a] for a in names))

    def share(stage, p, total):
        names = phases[p]
        buf, at = sum_bufs[stage][p], place(names, me)
        buf[at] = total
        copies = [
            pltpu.make_async_remote_copy(
                src_ref=buf.at[at],
                dst_ref=buf.at[at],
                send_sem=sum_send.at[stage, starts[p] + k],
                recv_sem=sum_recv.at[stage, starts[p] + at],
                device_id=ids,
                device_id_type=MESH,
            )
            for k, ids in enumerate(peers(names))
        ]
        for c in copies:
            c.start()
        return copies

    def collect(stage, p, copies):
        names = phases[p]
        buf = sum_bufs[stage][p]
        for ids in peers(names):
            at = place(names, ids)
            pltpu.make_async_copy(
                buf.at[at], buf.at[at], sum_recv.at[stage, starts[p] + at]
            ).wait()
        terms = [buf[k] for k in range(buf.shape[0])]
        while len(terms) > 1:
            terms = [sum(terms[k : k + 2][1:], terms[k]) for k in range(0, len(terms), 2)]
        for c in copies:
            c.wait_send()
        return terms[0]

    early = share(0, 0, jnp.concatenate([g00, g01, g11], axis=0))

    for g in range(clear):
        sweep_local(m1_v, g)
    third = {}

    def finish_second(b, z):
        here = pl.ds(b * blk, blk)
        xd_v[here] = z.astype(bf16)
        if b < faces:
            third[b] = face_copy(xd_v.at[here], nb2_v, 2, b)
            third[b].start()

    sweep_rest(d2_v, finish_second)
    g02 = jnp.zeros((1, rhs), f32)
    g12 = jnp.zeros((1, rhs), f32)
    g22 = jnp.zeros((1, rhs), f32)
    w_v[outside] = dot(s_v[outside], xd_v[...])
    for i in range(faces, nb):
        here = pl.ds(i * blk, blk)
        m = w_v[here]
        g02 = g02 + colsum(m * r0_v[here])
        g12 = g12 + colsum(m * m1_v[here])
        g22 = g22 + colsum(m * m)
    w_v[inside] = dot(s_v[inside], xd_v[...])
    for i in range(faces - 1, -1, -1):
        here = pl.ds(i * blk, blk)
        third[i ^ 1].wait_recv()
        m = w_v[here] + dot(c_v[i], nb2_v[i])
        g02 = g02 + colsum(m * r0_v[here])
        g12 = g12 + colsum(m * m1_v[here])
        g22 = g22 + colsum(m * m)

    final = share(1, 0, jnp.concatenate([g02, g12, g22], axis=0))
    early_sum = collect(0, 0, early)
    final_sum = collect(1, 0, final)
    for p in range(1, len(phases)):
        early = share(0, p, early_sum)
        final = share(1, p, final_sum)
        early_sum = collect(0, p, early)
        final_sum = collect(1, p, final)
    zero = jnp.zeros((1, rhs), f32)
    g00, g01, g11 = [early_sum[i : i + 1] for i in range(3)]
    g02, g12, g22 = [final_sum[i : i + 1] for i in range(3)]
    b2 = g00 + EPS
    start = jnp.sqrt(b2)
    h00 = (g01 + g00) / b2
    de = h00 - 1.0
    n1 = (g11 - 2.0 * de * g01 + de * de * g00) / b2
    h10 = jnp.sqrt(jnp.maximum(n1, 0.0) + EPS)
    s2 = start * h10
    r0q = g02 - de * (g01 + g00)
    m1q = g12 - de * (g11 + g01)
    h01 = r0q / (start * s2)
    h11 = (m1q - de * r0q) / (s2 * s2)
    qq = (
        g22 - 2.0 * de * (g12 + g02) + de * de * (g11 + 2.0 * g01 + g00)
    ) / (s2 * s2)
    k00 = g00 / b2
    k11 = n1 / (h10 * h10)
    k01 = (g01 - de * g00) / (start * s2)
    n2 = qq - 2.0 * (h01 * h01 + h11 * h11) + h01 * h01 * k00 + h11 * h11 * k11
    n2 = n2 + 2.0 * h01 * h11 * k01
    h21 = jnp.sqrt(jnp.maximum(n2, 0.0) + EPS)
    c0, c1, ratio = least_squares([[h00, h01], [h10, h11], [zero, h21]], start)
    a2 = c1 / s2
    coef_ref[...] = jnp.concatenate([c0 / start - de * a2, a2], axis=0)
    ratio_ref[...] = ratio
    for f in range(faces):
        first[f].wait_send()
        second[f].wait_send()
        third[f].wait_send()


def combine(x_ref, d1_ref, d2_ref, coef_ref, ratio_ref, out_hbm, ratio_out, out_v, sem):
    chunks = sem.shape[0]
    rows = x_ref.shape[0] // chunks
    copies = []
    for i in range(chunks):
        here = pl.ds(i * rows, rows)
        out_v[here] = (
            x_ref[here].astype(f32)
            + coef_ref[0:1] * d1_ref[here]
            + coef_ref[1:2] * d2_ref[here]
        )
        copies.append(pltpu.make_async_copy(out_v.at[here], out_hbm.at[here], sem.at[i]))
        copies[-1].start()
    ratio_out[...] = ratio_ref[...]
    for c in copies:
        c.wait()


def body(sizes, loads, start_guess, schur, coupling, diag_inverse, lower, upper):
    b, x, s, c, d, l, u = [
        v.reshape(v.shape[3:])
        for v in (loads, start_guess, schur, coupling, diag_inverse, lower, upper)
    ]
    n, r = b.shape
    nb, blk = d.shape[:2]
    faces = c.shape[0]
    groups = nb // GROUP
    gs = GROUP * blk
    chunks = 4
    phases = (AXES,)
    if math.prod(sizes.values()) > 32:
        phases = (("gx",), ("gy",), ("gz",))
    counts = [math.prod(sizes[a] for a in names) for names in phases]
    hbm_spec = pl.BlockSpec(memory_space=pltpu.HBM)
    vmem = pl.BlockSpec(memory_space=pltpu.VMEM)
    x0, d1, d2, coef, ratio = pl.pallas_call(
        functools.partial(kernel, sizes, phases),
        out_shape=(
            pltpu.VMEM((n, r), bf16),
            pltpu.VMEM((n, r), f32),
            pltpu.VMEM((n, r), f32),
            pltpu.VMEM((2, r), f32),
            pltpu.VMEM((1, r), f32),
        ),
        in_specs=[hbm_spec] * 7,
        out_specs=(vmem,) * 5,
        scratch_shapes=[
            pltpu.VMEM(s.shape, bf16),
            pltpu.VMEM(c.shape, bf16),
            pltpu.VMEM(d.shape, bf16),
            pltpu.VMEM(l.shape, bf16),
            pltpu.VMEM(u.shape, bf16),
            pltpu.VMEM((n, r), bf16),
            pltpu.VMEM((n, r), bf16),
            pltpu.VMEM((groups, gs, gs), bf16),
            pltpu.VMEM((groups, gs, blk), bf16),
            pltpu.VMEM((nb - 1, blk, blk), bf16),
            pltpu.VMEM((groups, gs, gs), bf16),
            pltpu.VMEM((groups, gs, blk), bf16),
            pltpu.VMEM((n, r), f32),
            pltpu.VMEM((n, r), f32),
            pltpu.VMEM((n, r), f32),
            pltpu.VMEM((n, 2 * r), bf16),
            pltpu.VMEM((n, 2 * r), bf16),
            pltpu.VMEM((faces, blk, r), bf16),
            pltpu.VMEM((faces, blk, r), bf16),
            pltpu.VMEM((faces, blk, r), bf16),
            pltpu.VMEM((faces, blk, r), bf16),
            [[pltpu.VMEM((count, 3, r), f32) for count in counts] for _ in range(2)],
            pltpu.SemaphoreType.DMA((chunks,)),
            pltpu.SemaphoreType.DMA((6,)),
            pltpu.SemaphoreType.DMA((3, faces)),
            pltpu.SemaphoreType.DMA((3, faces)),
            pltpu.SemaphoreType.DMA((2, sum(counts))),
            pltpu.SemaphoreType.DMA((2, sum(counts))),
        ],
        compiler_params=pltpu.CompilerParams(
            collective_id=0, has_side_effects=True, vmem_limit_bytes=60 << 20
        ),
    )(b, x, s, c, d, l, u)
    out, ratio = pl.pallas_call(
        combine,
        out_shape=(jax.ShapeDtypeStruct((n, r), f32), jax.ShapeDtypeStruct((1, r), f32)),
        in_specs=[vmem] * 5,
        out_specs=(hbm_spec, vmem),
        scratch_shapes=[pltpu.VMEM((n, r), f32), pltpu.SemaphoreType.DMA((chunks,))],
        compiler_params=pltpu.CompilerParams(vmem_limit_bytes=8 << 20),
    )(x0, d1, d2, coef, ratio)
    return out[None, None, None], ratio.reshape(r)


def solution(mesh):
    sizes = {a: mesh.shape[a] for a in AXES}
    deep = P("gx", "gy", "gz", None, None, None)
    flat = P("gx", "gy", "gz", None, None)
    return jax.shard_map(
        functools.partial(body, sizes),
        mesh=mesh,
        in_specs=(flat, flat, flat, deep, deep, deep, deep),
        out_specs=(flat, P()),
        check_vma=False,
    )
```

time: 41.9 us -> 38.1 us (0.909)
  other arithmetic: 2.68 us -> 0 us
  local copies, waits for them, and re-layouts: 1.86 us -> 0 us
  Pallas kernels: 36.5 us -> 37.3 us
    broadcast_in_dim x1 -> x0, other arithmetic: 2.68 us -> none  [body(): return (out[None, None, None], ratio.reshape(r))]
    unnamed x3 -> x0, local copies, waits for them, and re-layouts: 1.17 us -> none
    pallas_call x1 -> x2, Pallas kernels: 36.5 us -> 37.3 us  [the longest x1 35.8 us: body(): pl.pallas_call(functools.partial(kernel, sizes, phases), out_shape=(pltpu...]
    mul x1 -> x0, local copies, waits for them, and re-layouts: 0.69 us -> none  [body(): out = x.astype(f32) + coef[0:1] * d1 + coef[1:2] * d2]
where the time goes in v2:
time: 38.1 us; the launch traced here: 37.9 us
  Pallas kernels  37.3 us (98%)
  between operations  0.64 us (2%)
    pallas_call x1, Pallas kernels, body(): pl.pallas_call(functools.partial(kernel, sizes, phases), out_shape=(pltpu...  35.8 us
    pallas_call x1, Pallas kernels, body(): pl.pallas_call(combine, out_shape=(jax.ShapeDtypeStruct((n, r), f32), jax...  1.55 us

profile of v2, /device:TPU:0, one launch (start us, length us, event | category | flops | bytes accessed | tf_op | source)
XLA Modules:
  0.0 37.9 jit_solution(14109483044596286636)
XLA Ops:
  0.6 35.8 %shard_map.86 = (bf16[2048,128]{1,0:T(8,128)(2,1)S(1)}, f32[2048,128]{1,0:T(8,128)S(1)}, f32[2048,128]{1,0:T(8,128)S(1)}, f32[2,128]{1,0:T(2,128)S(1)}, f32[1,128]{1,0:T(1,128)S(1)}) custom-call(bf16[2048,128]{1,0:T(8,128)(2,1)} %bitcast.10, bf16[2048,128]{1,0:T(8,128)(2,1)} %bitcast.11, bf16[2048,2048]{1,0:T(8,128)(2,1)} %bitcast.9, ...), custom_call_target="tpu_custom_call" | custom-call | tf_op jit(solution)/shard_map/pallas_call | solution.py:412
  36.4 1.6 %shard_map.87 = (f32[2048,128]{1,0:T(8,128)}, f32[1,128]{1,0:T(1,128)}) custom-call(bf16[2048,128]{1,0:T(8,128)(2,1)S(1)} %get-tuple-element.9.x_ref, f32[2048,128]{1,0:T(8,128)S(1)} %get-tuple-element.10.d1_ref, f32[2048,128]{1,0:T(8,128)S(1)} %get-tuple-element.11.d2_ref, f32[2,128]{1,0:T(2,128)S(1)} %get-tuple-element.12.coef_ref, ...), custom_call_target="tpu_custom_call" | custom-call | tf_op jit(solution)/shard_map/pallas_call | solution.py:457

commit v3 on v2

--- a/solution.py
+++ b/solution.py
@@ -63,7 +63,6 @@
     rhs = b_v.shape[1]
     unknowns = b_v.shape[0]
     faces = c_v.shape[0]
-    fr = faces * blk
     groups = nb // GROUP
     chunks = s_sem.shape[0]
     rows = unknowns // chunks
@@ -146,13 +145,6 @@
     for k in range(nb - 1):
         e_v[k] = (-dot(d_v[k], u_v[k])).astype(bf16)
 
-    pl.semaphore_wait(barrier, greeted)
-    first = [
-        face_copy(x_hbm.at[pl.ds(f * blk, blk)], nb0_v, 0, f) for f in range(faces)
-    ]
-    for c in reversed(first):
-        c.start()
-
     for g in range(groups):
         a = g * GROUP
         for i in range(GROUP - 1, -1, -1):
@@ -174,6 +166,13 @@
     for i in range(chunks):
         s_loads[i].wait()
         r0_v[pl.ds(i * rows, rows)] = -dot(s_v[pl.ds(i * rows, rows)], x_v[...])
+        if i == 0:
+            pl.semaphore_wait(barrier, greeted)
+            first = [
+                face_copy(x_hbm.at[pl.ds(f * blk, blk)], nb0_v, 0, f) for f in range(faces)
+            ]
+            for c in reversed(first):
+                c.start()
     late[0].wait()
     late[1].wait()
     g00 = jnp.zeros((1, rhs), f32)
@@ -189,12 +188,12 @@
     gs = GROUP * blk
 
     def sweep_local(v_v, g):
-        cat = split(v_v[pl.ds(g * gs, gs)])
+        cat = v_v[pl.ds(g * gs, gs)].astype(bf16)
         for i in range(GROUP):
             here = pl.ds(g * gs + i * blk, blk)
             w = v_v[here]
             if i > 0:
-                w = w + fold(dot(t_v[g, pl.ds(i * blk, blk), pl.ds(0, i * blk)], cat[: i * blk]))
+                w = w + dot(t_v[g, pl.ds(i * blk, blk), pl.ds(0, i * blk)], cat[: i * blk])
             w_v[here] = w
 
     def sweep_rest(z_out, finish):
@@ -203,10 +202,10 @@
             rows_g = pl.ds(g * gs, gs)
             w = w_v[rows_g]
             if g > 0:
-                w = w + fold(dot(cf_v[g], last))
+                w = w + dot(cf_v[g], last)
             cat = split(w)
             wcat_v[rows_g] = cat
-            last = cat[gs - blk :]
+            last = cat[gs - blk :, :rhs]
         head = None
         for g in range(groups - 1, -1, -1):
             for i in range(GROUP):
@@ -219,15 +218,13 @@
                     )
                 )
                 if head is not None:
-                    z = z + fold(dot(cb_v[g, pl.ds(i * blk, blk)], head))
+                    z = z + dot(cb_v[g, pl.ds(i * blk, blk)], head)
                 z_out[pl.ds(b * blk, blk)] = z
                 finish(b, z)
                 if i == 0:
-                    following = split(z)
+                    following = z.astype(bf16)
             head = following
 
-    outside = pl.ds(fr, unknowns - fr)
-    inside = pl.ds(0, fr)
     clear = -(-faces // GROUP)
 
     for g in range(groups):
@@ -245,7 +242,7 @@
     sweep_rest(d1_v, finish_first)
     g01 = jnp.zeros((1, rhs), f32)
     g11 = jnp.zeros((1, rhs), f32)
-    m1_v[outside] = fold(dot(s_v[outside], xcat_v[...])) - r0_v[outside]
+    m1_v[...] = fold(dot(s_v[...], xcat_v[...])) - r0_v[...]
     for i in range(faces, nb):
         here = pl.ds(i * blk, blk)
         m = m1_v[here]
@@ -253,7 +250,6 @@
         g11 = g11 + colsum(m * m)
     for g in range(clear, groups):
         sweep_local(m1_v, g)
-    m1_v[inside] = fold(dot(s_v[inside], xcat_v[...])) - r0_v[inside]
     for i in range(faces - 1, -1, -1):
         here = pl.ds(i * blk, blk)
         second[i ^ 1].wait_recv()
@@ -317,14 +313,13 @@
     g02 = jnp.zeros((1, rhs), f32)
     g12 = jnp.zeros((1, rhs), f32)
     g22 = jnp.zeros((1, rhs), f32)
-    w_v[outside] = dot(s_v[outside], xd_v[...])
+    w_v[...] = dot(s_v[...], xd_v[...])
     for i in range(faces, nb):
         here = pl.ds(i * blk, blk)
         m = w_v[here]
         g02 = g02 + colsum(m * r0_v[here])
         g12 = g12 + colsum(m * m1_v[here])
         g22 = g22 + colsum(m * m)
-    w_v[inside] = dot(s_v[inside], xd_v[...])
     for i in range(faces - 1, -1, -1):
         here = pl.ds(i * blk, blk)
         third[i ^ 1].wait_recv()

time: 38.1 us -> 38.7 us (1.016)
  Pallas kernels: 37.3 us -> 37.8 us
    pallas_call x1, Pallas kernels: 35.8 us -> 36.2 us  [body(): pl.pallas_call(functools.partial(kernel, sizes, phases), out_shape=(pltpu...]
where the time goes in v3:
time: 38.7 us; the launch traced here: 38.6 us
  Pallas kernels  37.8 us (98%)
  between operations  0.8 us (2%)
    pallas_call x1, Pallas kernels, body(): pl.pallas_call(functools.partial(kernel, sizes, phases), out_shape=(pltpu...  36.2 us
    pallas_call x1, Pallas kernels, body(): pl.pallas_call(combine, out_shape=(jax.ShapeDtypeStruct((n, r), f32), jax...  1.55 us

profile of v3, /device:TPU:0, one launch (start us, length us, event | category | flops | bytes accessed | tf_op | source)
XLA Modules:
  0.0 38.6 jit_solution(1667665551313177081)
XLA Ops:
  0.6 36.2 %shard_map.86 = (bf16[2048,128]{1,0:T(8,128)(2,1)S(1)}, f32[2048,128]{1,0:T(8,128)S(1)}, f32[2048,128]{1,0:T(8,128)S(1)}, f32[2,128]{1,0:T(2,128)S(1)}, f32[1,128]{1,0:T(1,128)S(1)}) custom-call(bf16[2048,128]{1,0:T(8,128)(2,1)} %bitcast.10, bf16[2048,128]{1,0:T(8,128)(2,1)} %bitcast.11, bf16[2048,2048]{1,0:T(8,128)(2,1)} %bitcast.9, ...), custom_call_target="tpu_custom_call" | custom-call | tf_op jit(solution)/shard_map/pallas_call | solution.py:407
  36.9 1.6 %shard_map.87 = (f32[2048,128]{1,0:T(8,128)}, f32[1,128]{1,0:T(1,128)}) custom-call(bf16[2048,128]{1,0:T(8,128)(2,1)S(1)} %get-tuple-element.9.x_ref, f32[2048,128]{1,0:T(8,128)S(1)} %get-tuple-element.10.d1_ref, f32[2048,128]{1,0:T(8,128)S(1)} %get-tuple-element.11.d2_ref, f32[2,128]{1,0:T(2,128)S(1)} %get-tuple-element.12.coef_ref, ...), custom_call_target="tpu_custom_call" | custom-call | tf_op jit(solution)/shard_map/pallas_call | solution.py:452

commit v4 on v3

--- a/solution.py
+++ b/solution.py
@@ -225,6 +225,8 @@
                     following = z.astype(bf16)
             head = following
 
+    outside = pl.ds(faces * blk, unknowns - faces * blk)
+    inside = pl.ds(0, faces * blk)
     clear = -(-faces // GROUP)
 
     for g in range(groups):
@@ -242,7 +244,7 @@
     sweep_rest(d1_v, finish_first)
     g01 = jnp.zeros((1, rhs), f32)
     g11 = jnp.zeros((1, rhs), f32)
-    m1_v[...] = fold(dot(s_v[...], xcat_v[...])) - r0_v[...]
+    m1_v[outside] = fold(dot(s_v[outside], xcat_v[...])) - r0_v[outside]
     for i in range(faces, nb):
         here = pl.ds(i * blk, blk)
         m = m1_v[here]
@@ -250,6 +252,7 @@
         g11 = g11 + colsum(m * m)
     for g in range(clear, groups):
         sweep_local(m1_v, g)
+    m1_v[inside] = fold(dot(s_v[inside], xcat_v[...])) - r0_v[inside]
     for i in range(faces - 1, -1, -1):
         here = pl.ds(i * blk, blk)
         second[i ^ 1].wait_recv()
@@ -313,13 +316,14 @@
     g02 = jnp.zeros((1, rhs), f32)
     g12 = jnp.zeros((1, rhs), f32)
     g22 = jnp.zeros((1, rhs), f32)
-    w_v[...] = dot(s_v[...], xd_v[...])
+    w_v[outside] = dot(s_v[outside], xd_v[...])
     for i in range(faces, nb):
         here = pl.ds(i * blk, blk)
         m = w_v[here]
         g02 = g02 + colsum(m * r0_v[here])
         g12 = g12 + colsum(m * m1_v[here])
         g22 = g22 + colsum(m * m)
+    w_v[inside] = dot(s_v[inside], xd_v[...])
     for i in range(faces - 1, -1, -1):
         here = pl.ds(i * blk, blk)
         third[i ^ 1].wait_recv()

time: 38.7 us -> 37.3 us (0.964)
  Pallas kernels: 37.8 us -> 36.5 us
    pallas_call x1, Pallas kernels: 36.2 us -> 35 us  [body(): pl.pallas_call(functools.partial(kernel, sizes, phases), out_shape=(pltpu...]
where the time goes in v4:
time: 37.3 us; the launch traced here: 37.2 us
  Pallas kernels  36.5 us (98%)
  between operations  0.64 us (2%)
    pallas_call x1, Pallas kernels, body(): pl.pallas_call(functools.partial(kernel, sizes, phases), out_shape=(pltpu...  35 us
    pallas_call x1, Pallas kernels, body(): pl.pallas_call(combine, out_shape=(jax.ShapeDtypeStruct((n, r), f32), jax...  1.55 us

profile of v4, /device:TPU:0, one launch (start us, length us, event | category | flops | bytes accessed | tf_op | source)
XLA Modules:
  0.0 37.2 jit_solution(5237075281165790688)
XLA Ops:
  0.6 35.0 %shard_map.86 = (bf16[2048,128]{1,0:T(8,128)(2,1)S(1)}, f32[2048,128]{1,0:T(8,128)S(1)}, f32[2048,128]{1,0:T(8,128)S(1)}, f32[2,128]{1,0:T(2,128)S(1)}, f32[1,128]{1,0:T(1,128)S(1)}) custom-call(bf16[2048,128]{1,0:T(8,128)(2,1)} %bitcast.10, bf16[2048,128]{1,0:T(8,128)(2,1)} %bitcast.11, bf16[2048,2048]{1,0:T(8,128)(2,1)} %bitcast.9, ...), custom_call_target="tpu_custom_call" | custom-call | tf_op jit(solution)/shard_map/pallas_call | solution.py:411
  35.6 1.6 %shard_map.87 = (f32[2048,128]{1,0:T(8,128)}, f32[1,128]{1,0:T(1,128)}) custom-call(bf16[2048,128]{1,0:T(8,128)(2,1)S(1)} %get-tuple-element.9.x_ref, f32[2048,128]{1,0:T(8,128)S(1)} %get-tuple-element.10.d1_ref, f32[2048,128]{1,0:T(8,128)S(1)} %get-tuple-element.11.d2_ref, f32[2,128]{1,0:T(2,128)S(1)} %get-tuple-element.12.coef_ref, ...), custom_call_target="tpu_custom_call" | custom-call | tf_op jit(solution)/shard_map/pallas_call | solution.py:456
